TPU v7x, 512 devices: a whole 4x4x16 slice. The times are simulated.
512 devices in a mesh: lag: 64 (over z, y), par: 8 (over x, core).
Axes of the slice: x: 4, y: 4, z: 16, core: 2. Of those that a mesh axis runs over, the one named last changes fastest.
Arguments:
- prior_rows: bfloat16 [64, 512, 16384], P('lag', None, 'par'), may hold values from -0.0625 to 0.0625
- raw_rows: bfloat16 [64, 512, 16384], P('lag', None, 'par'), may hold values from -6 to 6
Outputs:
- diag_zero: float32 [64, 512, 512], P('lag', 'par')
- diag_one: float32 [64, 512, 512], P('lag', 'par')
All inputs are finite; a program needn't handle non-finite values.
Results may differ from a plain program's by a relative error of at most 0.0003.
Values may be sent and summed in bfloat16 or wider, within the bound.
No kernel may reach another device: no remote copies, remote signals or barrier semaphores. Data moves between devices by JAX's collectives and lax.ppermute only.
A program may use at most 64 MiB of HBM per device.

v0:
```python
import jax
import jax.numpy as jnp
import numpy as np
from jax import lax
from jax.experimental import pallas as pl
from jax.experimental.pallas import tpu as pltpu
from jax.sharding import Mesh, PartitionSpec as P


F32 = jnp.float32
F16 = jnp.float16
NT = (((1,), (1,)), ((), ()))
LAG = ("zh", "zl", "y")
PAR = ("x", "core")
VMEM = pl.BlockSpec(memory_space=pltpu.VMEM)
STEPS = 4


def near(value):
    return pltpu.with_memory_space_constraint(value, pltpu.VMEM)


def far(value):
    return pltpu.with_memory_space_constraint(value, pltpu.HBM)


def call(kernel, out_shape, *args, scratch=()):
    return pl.pallas_call(
        kernel,
        out_shape=out_shape,
        scratch_shapes=scratch,
        in_specs=[VMEM] * len(args),
        out_specs=jax.tree.map(lambda _: VMEM, out_shape),
        compiler_params=pltpu.CompilerParams(vmem_limit_bytes=6 * 2**20),
    )(*[near(arg) for arg in args])


def shape(*dims):
    return pltpu.VMEM(dims, F32)


def result(*dims):
    return jax.ShapeDtypeStruct(dims, F32)


def exponent_of(value):
    top = jnp.max(jnp.max(jnp.abs(value), axis=0, keepdims=True), axis=1, keepdims=True)
    return jnp.floor(jnp.log2(jnp.maximum(top, 1e-30)))


LEVEL = 3.3


def encode(value, exponent):
    size = jnp.abs(value) * jnp.exp2(7.0 - exponent)
    binade = jnp.floor(jnp.log2(jnp.maximum(size, 1.0)))
    place = LEVEL * (binade + size * jnp.exp2(-binade))
    whole = jnp.floor(place)
    code = jnp.exp2(whole - 14.0) * (1.0 + (place - whole))
    return jnp.where(value < 0, -code, code)


def decode(code, exponent):
    size = jnp.abs(code)
    whole = jnp.floor(jnp.log2(jnp.maximum(size, 2.0**-14)))
    place = (whole + 13.0 + size * jnp.exp2(-whole)) * (1.0 / LEVEL)
    binade = jnp.maximum(jnp.floor(place) - 1.0, 0.0)
    value = (place - binade) * jnp.exp2(binade + exponent - 7.0)
    return jnp.where(code < 0, -value, value)


def pack_rows(tile, out):
    exponent = exponent_of(tile)
    tail = jnp.broadcast_to(exponent, (8, 128))
    sent = tile * jnp.exp2(14.0 - exponent)
    for x in range(4):
        for c in range(2):
            first = x * 128 + c * 64
            groups = [sent[first + i * 8 : first + (i + 1) * 8] for i in range(8)]
            out[x, c] = jnp.concatenate(groups + [tail], axis=1)


def summed_rows(parts):
    groups = [None] * 8
    for part in parts:
        scale = jnp.exp2(part[:, 4096:] - 14.0)
        scale = jnp.concatenate([scale] * 4, axis=1)
        for i in range(8):
            group = part[:, i * 512 : (i + 1) * 512] * scale
            groups[i] = group if groups[i] is None else groups[i] + group
    return jnp.concatenate(groups, axis=0)


def pack_blocks(tile, out):
    exponent = exponent_of(tile)
    tail = jnp.broadcast_to(exponent, (8, 128))
    sent = tile * jnp.exp2(14.0 - exponent)
    for x in range(4):
        for c in range(2):
            for y in range(4):
                first = x * 128 + c * 64 + y * 16
                top, bottom = sent[first : first + 8], sent[first + 8 : first + 16]
                out[y, x, c] = jnp.concatenate([top, bottom, tail], axis=1)


def unpack(sent):
    scale = jnp.exp2(sent[:, 1024:] - 14.0)
    scale = jnp.concatenate([scale] * 4, axis=1)
    return sent[:, :512] * scale, sent[:, 512:1024] * scale


def summed_blocks(parts):
    top, bottom = unpack(parts[0])
    for part in parts[1:]:
        more_top, more_bottom = unpack(part)
        top, bottom = top + more_top, bottom + more_bottom
    return jnp.concatenate([top, bottom], axis=0)


def tile_zero_kernel(prior, raw, out, prior_near, raw_near, total, sems):
    width = 2048 // STEPS
    copies = []
    for step in range(STEPS):
        group = []
        for i in range(4):
            source, target = (prior, prior_near) if i < 2 else (raw, raw_near)
            piece = (pl.ds(i % 2 * 256, 256), pl.ds(step * width, width))
            group.append(pltpu.make_async_copy(source.at[piece], target.at[piece], sems.at[step * 4 + i]))
        copies.append(group)
    for group in copies:
        for copy in group:
            copy.start()
    for step, group in enumerate(copies):
        for copy in group:
            copy.wait()
        columns = slice(step * width, (step + 1) * width)
        part = lax.dot_general(prior_near[:, columns], raw_near[:, columns], NT, preferred_element_type=F32)
        if step == 0:
            total[...] = part
        else:
            total[...] += part
    pack_rows(total[...], out)


def tile_one_kernel(prior, raw_next, prior_last, raw, out):
    def form(left, right):
        pack_blocks(lax.dot_general(left[...], right[...], NT, preferred_element_type=F32), out)

    core = lax.axis_index("core")
    pl.when(core == 0)(lambda: form(prior, raw_next))
    pl.when(core == 1)(lambda: form(prior_last, raw))


def add_kernel(parts, *outs):
    *outs, whole = outs
    whole[...] = summed_rows([parts[x, c] for x in range(4) for c in range(2)])
    place = lax.axis_index("y")
    for d, out in enumerate(outs):
        out[...] = whole[pl.ds(pl.multiple_of((place + d) % 4 * 16, 16), 16)]


def plane_prefix_kernel(zero_a, zero_b, zero_c, zero_d, one, out, zero):
    place = lax.axis_index("y")
    for d, part in enumerate((zero_a, zero_b, zero_c, zero_d)):
        zero[(place + 4 - d) % 4] = part[...]
    zeros, ones, late = [], [], None
    for lag in range(4):
        zeros.append(zero[lag] if lag == 0 else zeros[-1] + zero[lag])
        here, after = (summed_blocks([one[lag, x, c] for x in range(4)]) for c in range(2))
        if lag == 0:
            late, total = after, here + after
        else:
            ones.append(total + after)
            total = total + here + after
    ones.append(total)
    first = 0
    for i, parts in enumerate((zeros, ones, [late])):
        value = jnp.concatenate(parts, axis=0)
        exponent = exponent_of(value)
        value = encode(value, exponent)
        height = value.shape[0]
        for zl in range(4):
            out[zl, first : first + height] = value[:, zl * 128 : (zl + 1) * 128]
            out[zl, 144 + i * 8 : 152 + i * 8] = jnp.broadcast_to(exponent, (8, 128))
        first += height


def block_prefix_kernel(planes, local, total):
    def read(zl, i, first):
        exponent = planes[zl, 144 + i * 8 : 152 + i * 8]
        exponent = jnp.concatenate([exponent, exponent], axis=0)
        return decode(planes[zl, first : first + 16], exponent)

    zero, one = jnp.zeros((16, 128), F32), jnp.zeros((16, 128), F32)
    lates = [read(zl, 2, 128) for zl in range(4)]
    for zl in range(4):
        for lag in range(4):
            here_zero = zero + read(zl, 0, lag * 16)
            here_one = one + read(zl, 1, 64 + lag * 16)
            local[zl * 4 + lag, 0:16] = here_zero
            local[zl * 4 + lag, 16:32] = here_one + lates[zl + 1] if lag == 3 and zl < 3 else here_one
        zero, one = here_zero, here_one
    total[0:16], total[16:32], total[32:48] = zero, one, lates[0]


def sum_kernel(total, other, out):
    out[0:32] = total[0:32] + other[0:32]
    out[32:48] = total[32:48]


def finish_kernel(local, early, back, crossed, own, out):
    place = lax.axis_index("zh")

    def pick(chosen, ref, first, last):
        return jnp.where(chosen, ref[first:last], 0.0)

    earlier = pick(place == 1, early, 0, 32) + pick(place >= 2, crossed, 0, 32) + pick(place == 3, own, 0, 32)
    late = pick(place == 0, early, 32, 48) + pick(place == 1, back, 32, 48) + pick(place == 2, own, 32, 48)
    for i in range(16):
        out[i] = local[i] + earlier
    out[15, 16:32] = local[15, 16:32] + earlier[16:32] + late


def split_kernel(rows, zero, one):
    for zl in range(4):
        for y in range(4):
            here, there = slice(y * 16, (y + 1) * 16), slice(zl * 128, (zl + 1) * 128)
            zero[0, here, there] = rows[zl * 4 + y, 0:16]
            one[0, here, there] = rows[zl * 4 + y, 16:32]


def exchange(value, axes):
    return lax.all_to_all(value, axes, 0, 0, tiled=True)


def exchange_short(value, axes):
    return exchange(value.astype(F16), axes).astype(F32)


def body(prior_rows, raw_rows):
    prior, raw = prior_rows[0], raw_rows[0]
    device = np.arange(512).reshape(64, 4, 2)
    down = [(int(device[l + 1, x, 0]), int(device[l, x, 0])) for l in range(63) for x in range(4)]
    up = [(int(device[l, x, 1]), int(device[l + 1, x, 1])) for l in range(63) for x in range(4)]
    raw_next = lax.ppermute(raw, LAG + PAR, down)
    prior_last = lax.ppermute(prior, LAG + PAR, up)

    full = pltpu.VMEM((512, 2048), jnp.bfloat16)
    zero, prior, raw = pl.pallas_call(
        tile_zero_kernel,
        out_shape=(shape(4, 2, 8, 4224), full, full),
        in_specs=[pl.BlockSpec(memory_space=pltpu.HBM)] * 2,
        out_specs=(VMEM,) * 3,
        scratch_shapes=[pltpu.VMEM((512, 512), F32), pltpu.SemaphoreType.DMA((STEPS * 4,))],
        compiler_params=pltpu.CompilerParams(vmem_limit_bytes=8 * 2**20),
    )(far(prior), far(raw))
    zero = exchange_short(zero.reshape(8, 8, 4224), PAR).reshape(4, 2, 8, 4224)
    rows = call(add_kernel, (shape(16, 512),) * 4, zero, scratch=(shape(64, 512),))
    zero = [rows[0]]
    for d in range(1, 4):
        zero.append(lax.ppermute(rows[d], "y", [(i, (i + d) % 4) for i in range(4)]))

    one = call(tile_one_kernel, shape(4, 4, 2, 8, 1152), prior, raw_next, prior_last, raw)
    one = exchange_short(one.reshape(32, 8, 1152), ("y", "x", "core")).reshape(4, 4, 2, 8, 1152)

    planes = exchange_short(call(plane_prefix_kernel, shape(4, 168, 128), *zero, one, scratch=(shape(4, 16, 512),)), "zl")
    local, total = call(block_prefix_kernel, (shape(16, 32, 128), shape(48, 128)), planes)
    early = lax.ppermute(total, "zh", [(0, 1), (1, 0)])
    back = lax.ppermute(total, "zh", [(2, 1)])
    both = call(sum_kernel, shape(48, 128), total, early)
    crossed = lax.ppermute(both, "zh", [(1, 2), (0, 3)])
    own = lax.ppermute(total, "zh", [(2, 3), (3, 2)])
    rows = call(finish_kernel, shape(16, 32, 128), local, early, back, crossed, own)
    return tuple(call(split_kernel, (result(1, 64, 512), result(1, 64, 512)), exchange(rows, ("zl", "y"))))


def solution(mesh):
    chips = Mesh(mesh.devices.reshape(4, 4, 4, 4, 2), LAG + PAR)
    in_specs = (P(LAG, None, PAR), P(LAG, None, PAR))
    out_specs = (P(LAG, PAR, None), P(LAG, PAR, None))
    return jax.shard_map(body, mesh=chips, in_specs=in_specs, out_specs=out_specs, check_vma=False)
```

profile of v0, /device:TPU:2, one launch (start us, length us, event | category | flops | bytes accessed | tf_op | source)
XLA Modules:
  0.0 111.1 jit_solution(3438469604458200126)
XLA Ops:
  0.6 1.3 %collective-permute-start.3 = (bf16[512,2048]{1,0:T(8,128)(2,1)}, bf16[512,2048]{1,0:T(8,128)(2,1)S(1)}, u32[]{:S(2)}, u32[]{:S(2)}) collective-permute-start(bf16[512,2048]{1,0:T(8,128)(2,1)} %bitcast.10), channel_id=1, source_target_pairs={{8,0},{10,2},{12,4},{14,6},{16,8},{18,10},{20,12},{22,14},{24,16},... | collective-permute-start | bytes 6291464 | tf_op jit(solution)/shard_map/ppermute | solution.py:245
  1.9 2.0 %collective-permute-start.4 = (bf16[512,2048]{1,0:T(8,128)(2,1)}, bf16[512,2048]{1,0:T(8,128)(2,1)}, u32[]{:S(2)}, u32[]{:S(2)}) collective-permute-start(bf16[512,2048]{1,0:T(8,128)(2,1)} %bitcast.12), channel_id=1, source_target_pairs={{1,9},{3,11},{5,13},{7,15},{9,17},{11,19},{13,21},{15,23},{17,25},... | collective-permute-start | bytes 6291464 | tf_op jit(solution)/shard_map/ppermute | solution.py:246
  3.9 3.1 %shard_map.41 = (f32[4,2,8,4224]{3,2,1,0:T(8,128)S(1)}, bf16[512,2048]{1,0:T(8,128)(2,1)S(1)}, bf16[512,2048]{1,0:T(8,128)(2,1)S(1)}) custom-call(bf16[512,2048]{1,0:T(8,128)(2,1)} %bitcast.13, bf16[512,2048]{1,0:T(8,128)(2,1)} %bitcast.11), custom_call_target="tpu_custom_call" | custom-call | tf_op jit(solution)/shard_map/pallas_call | solution.py:249
  7.0 0.0 copy-start
  7.0 1.3 %copy-done = bf16[512,2048]{1,0:T(8,128)(2,1)} copy-done((bf16[512,2048]{1,0:T(8,128)(2,1)}, bf16[512,2048]{1,0:T(8,128)(2,1)S(1)}, u32[]{:S(2)}) %copy-start) | copy-done | bytes 2097176
  8.3 0.0 copy-start.2
  8.3 1.4 %copy-done.2 = bf16[512,2048]{1,0:T(8,128)(2,1)} copy-done((bf16[512,2048]{1,0:T(8,128)(2,1)}, bf16[512,2048]{1,0:T(8,128)(2,1)S(1)}, u32[]{:S(2)}) %copy-start.2) | copy-done | bytes 2097176
  9.7 0.9 convert_element_type.20
  10.5 9.3 %all-to-all-start = ((f16[8,8,4224]{2,1,0:T(8,128)(2,1)}), f16[8,8,4224]{2,1,0:T(8,128)(2,1)S(1)}, u32[]{:S(2)}, u32[]{:S(2)}) async-start(f16[8,8,4224]{2,1,0:T(8,128)(2,1)} %bitcast.2), calls=%async_computation | async-start | bytes 1081344 | tf_op jit(solution)/shard_map/all_to_all | solution.py:233
  19.9 8.9 %collective-permute-done.3.raw_next = bf16[512,2048]{1,0:T(8,128)(2,1)S(1)} collective-permute-done((bf16[512,2048]{1,0:T(8,128)(2,1)}, bf16[512,2048]{1,0:T(8,128)(2,1)S(1)}, u32[]{:S(2)}, u32[]{:S(2)}) %collective-permute-start.3) | collective-permute-done | bytes 2097184 | tf_op jit(solution)/shard_map/ppermute | solution.py:245
  28.8 0.0 collective-permute-done.4.prior_last
  28.8 0.0 copy-start.1
  28.8 1.6 %copy-done.1 = bf16[512,2048]{1,0:T(8,128)(2,1)S(1)} copy-done((bf16[512,2048]{1,0:T(8,128)(2,1)S(1)}, bf16[512,2048]{1,0:T(8,128)(2,1)}, u32[]{:S(2)}) %copy-start.1) | copy-done | bytes 2097176
  30.4 0.0 copy-start.3
  30.4 1.6 %copy-done.3 = bf16[512,2048]{1,0:T(8,128)(2,1)S(1)} copy-done((bf16[512,2048]{1,0:T(8,128)(2,1)S(1)}, bf16[512,2048]{1,0:T(8,128)(2,1)}, u32[]{:S(2)}) %copy-start.3) | copy-done | bytes 2097176
  32.0 3.0 %shard_map.43 = f32[4,4,2,8,1152]{4,3,2,1,0:T(8,128)S(1)} custom-call(bf16[512,2048]{1,0:T(8,128)(2,1)S(1)} %copy-done.1, bf16[512,2048]{1,0:T(8,128)(2,1)S(1)} %collective-permute-done.3.raw_next, bf16[512,2048]{1,0:T(8,128)(2,1)} %collective-permute-done.4.prior_last, bf16[512,2048]{1,0:T(8,128)(2,1)S(1)} %copy-done.3), custom_call_target="tpu_custom_call" | custom-call | tf_op jit(solution)/shard_map/pallas_call | solution.py:28
  35.0 0.9 convert_element_type.22
  35.9 0.0 all-to-all-done
  35.9 9.6 %all-to-all-start.1 = ((f16[32,8,1152]{2,1,0:T(8,128)(2,1)}), f16[32,8,1152]{2,1,0:T(8,128)(2,1)S(1)}, u32[]{:S(2)}, u32[]{:S(2)}) async-start(f16[32,8,1152]{2,1,0:T(8,128)(2,1)} %bitcast.4), calls=%async_computation.1 | async-start | bytes 1179648 | tf_op jit(solution)/shard_map/all_to_all | solution.py:233
  45.5 0.1 convert.2.parts
  45.5 0.1 shard_map.42
  45.6 3.4 %collective-permute-start = (f32[16,512]{1,0:T(8,128)S(1)}, f32[16,512]{1,0:T(8,128)S(1)}, u32[]{:S(2)}, u32[]{:S(2)}) collective-permute-start(f32[16,512]{1,0:T(8,128)S(1)} %get-tuple-element.13), channel_id=1, source_target_pairs={{0,8},{8,16},{16,24},{24,0},{1,9},{9,17},{17,25},{25,1},{2,10},{10... | collective-permute-start | bytes 98312 | tf_op jit(solution)/shard_map/ppermute | solution.py:261
  49.0 4.6 %collective-permute-start.1 = (f32[16,512]{1,0:T(8,128)S(1)}, f32[16,512]{1,0:T(8,128)S(1)}, u32[]{:S(2)}, u32[]{:S(2)}) collective-permute-start(f32[16,512]{1,0:T(8,128)S(1)} %get-tuple-element.14), channel_id=1, source_target_pairs={{0,16},{8,24},{16,0},{24,8},{1,17},{9,25},{17,1},{25,9},{2,18},{10... | collective-permute-start | bytes 98312 | tf_op jit(solution)/shard_map/ppermute | solution.py:261
  53.7 3.3 %collective-permute-start.2 = (f32[16,512]{1,0:T(8,128)S(1)}, f32[16,512]{1,0:T(8,128)S(1)}, u32[]{:S(2)}, u32[]{:S(2)}) collective-permute-start(f32[16,512]{1,0:T(8,128)S(1)} %get-tuple-element.15), channel_id=1, source_target_pairs={{0,24},{8,0},{16,8},{24,16},{1,25},{9,1},{17,9},{25,17},{2,26},{10... | collective-permute-start | bytes 98312 | tf_op jit(solution)/shard_map/ppermute | solution.py:261
  57.0 0.0 all-to-all-done.1
  57.0 0.1 convert.3.one
  57.1 0.0 collective-permute-done.zero_b
  57.1 0.1 collective-permute-done.1.zero_c
  57.2 2.2 %collective-permute-done.2.zero_d = f32[16,512]{1,0:T(8,128)S(1)} collective-permute-done((f32[16,512]{1,0:T(8,128)S(1)}, f32[16,512]{1,0:T(8,128)S(1)}, u32[]{:S(2)}, u32[]{:S(2)}) %collective-permute-start.2) | collective-permute-done | bytes 32800 | tf_op jit(solution)/shard_map/ppermute | solution.py:261
  59.5 0.4 shard_map.44
  59.9 13.6 %all_to_all.20 = f16[4,168,128]{2,1,0:T(8,128)(2,1)S(1)} all-to-all(f16[4,168,128]{2,1,0:T(8,128)(2,1)S(1)} %convert_element_type.24), channel_id=1, replica_groups=mesh['zh'=4,'zl'=4,'y'=4,'x'=4,'core'=2] {'zl'}, dimensions={0} | all-to-all | bytes 344064 | tf_op jit(solution)/shard_map/all_to_all | solution.py:233
  73.5 0.2 shard_map.45
  73.8 9.1 %collective-permute-start.5 = (f32[48,128]{1,0:T(8,128)S(1)}, f32[48,128]{1,0:T(8,128)S(1)}, u32[]{:S(2)}, u32[]{:S(2)}) collective-permute-start(f32[48,128]{1,0:T(8,128)S(1)} %get-tuple-element.19.total), channel_id=1, source_target_pairs={{0,128},{128,0},{1,129},{129,1},{2,130},{130,2},{3,131},{131,3},{4... | collective-permute-start | bytes 73736 | tf_op jit(solution)/shard_map/ppermute | solution.py:268
  82.9 0.7 collective-permute-start.6
  83.5 0.7 collective-permute-start.8
  84.2 1.2 %collective-permute-done.5.other.early = f32[48,128]{1,0:T(8,128)S(1)} collective-permute-done((f32[48,128]{1,0:T(8,128)S(1)}, f32[48,128]{1,0:T(8,128)S(1)}, u32[]{:S(2)}, u32[]{:S(2)}) %collective-permute-start.5) | collective-permute-done | bytes 24608 | tf_op jit(solution)/shard_map/ppermute | solution.py:268
  85.5 9.1 %collective-permute-start.7 = (f32[48,128]{1,0:T(8,128)S(1)}, f32[48,128]{1,0:T(8,128)S(1)}, u32[]{:S(2)}, u32[]{:S(2)}) collective-permute-start(f32[48,128]{1,0:T(8,128)S(1)} %shard_map.46), channel_id=1, source_target_pairs={{128,256},{0,384},{129,257},{1,385},{130,258},{2,386},{131,259},{3... | collective-permute-start | bytes 73736 | tf_op jit(solution)/shard_map/ppermute | solution.py:271
  94.6 0.0 collective-permute-done.6.back
  94.6 0.0 collective-permute-done.8.own
  94.6 1.5 %collective-permute-done.7.crossed = f32[48,128]{1,0:T(8,128)S(1)} collective-permute-done((f32[48,128]{1,0:T(8,128)S(1)}, f32[48,128]{1,0:T(8,128)S(1)}, u32[]{:S(2)}, u32[]{:S(2)}) %collective-permute-start.7) | collective-permute-done | bytes 24608 | tf_op jit(solution)/shard_map/ppermute | solution.py:271
  96.1 14.3 %all_to_all.21.rows = f32[16,32,128]{2,1,0:T(8,128)S(1)} all-to-all(f32[16,32,128]{2,1,0:T(8,128)S(1)} %shard_map.47), channel_id=1, replica_groups=mesh['zh'=4,'zl'=4,'y'=4,'x'=4,'core'=2] {'zl','y'}, dimensions={0} | all-to-all | bytes 524288 | tf_op jit(solution)/shard_map/all_to_all | solution.py:233
  110.4 0.7 shard_map.48
  (4 shorter events, 0.1 us)
Async XLA Ops:
  0.6 28.1 %collective-permute-start.3 = (bf16[512,2048]{1,0:T(8,128)(2,1)}, bf16[512,2048]{1,0:T(8,128)(2,1)S(1)}, u32[]{:S(2)}, u32[]{:S(2)}) collective-permute-start(bf16[512,2048]{1,0:T(8,128)(2,1)} %bitcast.10), channel_id=1, source_target_pairs={{8,0},{10,2},{12,4},{14,6},{16,8},{18,10},{20,12},{22,14},{24,16},... | collective-permute-start | bytes 6291464 | tf_op jit(solution)/shard_map/ppermute | solution.py:245
  1.9 26.8 %collective-permute-start.4 = (bf16[512,2048]{1,0:T(8,128)(2,1)}, bf16[512,2048]{1,0:T(8,128)(2,1)}, u32[]{:S(2)}, u32[]{:S(2)}) collective-permute-start(bf16[512,2048]{1,0:T(8,128)(2,1)} %bitcast.12), channel_id=1, source_target_pairs={{1,9},{3,11},{5,13},{7,15},{9,17},{11,19},{13,21},{15,23},{17,25},... | collective-permute-start | bytes 6291464 | tf_op jit(solution)/shard_map/ppermute | solution.py:246
  7.0 1.3 %copy-start = (bf16[512,2048]{1,0:T(8,128)(2,1)}, bf16[512,2048]{1,0:T(8,128)(2,1)S(1)}, u32[]{:S(2)}) copy-start(bf16[512,2048]{1,0:T(8,128)(2,1)S(1)} %get-tuple-element.16.prior) | copy-start | bytes 6291460
  8.3 1.4 %copy-start.2 = (bf16[512,2048]{1,0:T(8,128)(2,1)}, bf16[512,2048]{1,0:T(8,128)(2,1)S(1)}, u32[]{:S(2)}) copy-start(bf16[512,2048]{1,0:T(8,128)(2,1)S(1)} %get-tuple-element.17.raw) | copy-start | bytes 6291460
  10.5 25.4 %all-to-all-start = ((f16[8,8,4224]{2,1,0:T(8,128)(2,1)}), f16[8,8,4224]{2,1,0:T(8,128)(2,1)S(1)}, u32[]{:S(2)}, u32[]{:S(2)}) async-start(f16[8,8,4224]{2,1,0:T(8,128)(2,1)} %bitcast.2), calls=%async_computation | async-start | bytes 1081344 | tf_op jit(solution)/shard_map/all_to_all | solution.py:233
  28.8 1.6 %copy-start.1 = (bf16[512,2048]{1,0:T(8,128)(2,1)S(1)}, bf16[512,2048]{1,0:T(8,128)(2,1)}, u32[]{:S(2)}) copy-start(bf16[512,2048]{1,0:T(8,128)(2,1)} %copy-done) | copy-start | bytes 6291460
  30.4 1.6 %copy-start.3 = (bf16[512,2048]{1,0:T(8,128)(2,1)S(1)}, bf16[512,2048]{1,0:T(8,128)(2,1)}, u32[]{:S(2)}) copy-start(bf16[512,2048]{1,0:T(8,128)(2,1)} %copy-done.2) | copy-start | bytes 6291460
  35.9 21.1 %all-to-all-start.1 = ((f16[32,8,1152]{2,1,0:T(8,128)(2,1)}), f16[32,8,1152]{2,1,0:T(8,128)(2,1)S(1)}, u32[]{:S(2)}, u32[]{:S(2)}) async-start(f16[32,8,1152]{2,1,0:T(8,128)(2,1)} %bitcast.4), calls=%async_computation.1 | async-start | bytes 1179648 | tf_op jit(solution)/shard_map/all_to_all | solution.py:233
  45.6 11.5 %collective-permute-start = (f32[16,512]{1,0:T(8,128)S(1)}, f32[16,512]{1,0:T(8,128)S(1)}, u32[]{:S(2)}, u32[]{:S(2)}) collective-permute-start(f32[16,512]{1,0:T(8,128)S(1)} %get-tuple-element.13), channel_id=1, source_target_pairs={{0,8},{8,16},{16,24},{24,0},{1,9},{9,17},{17,25},{25,1},{2,10},{10... | collective-permute-start | bytes 98312 | tf_op jit(solution)/shard_map/ppermute | solution.py:261
  49.0 8.2 %collective-permute-start.1 = (f32[16,512]{1,0:T(8,128)S(1)}, f32[16,512]{1,0:T(8,128)S(1)}, u32[]{:S(2)}, u32[]{:S(2)}) collective-permute-start(f32[16,512]{1,0:T(8,128)S(1)} %get-tuple-element.14), channel_id=1, source_target_pairs={{0,16},{8,24},{16,0},{24,8},{1,17},{9,25},{17,1},{25,9},{2,18},{10... | collective-permute-start | bytes 98312 | tf_op jit(solution)/shard_map/ppermute | solution.py:261
  53.7 5.8 %collective-permute-start.2 = (f32[16,512]{1,0:T(8,128)S(1)}, f32[16,512]{1,0:T(8,128)S(1)}, u32[]{:S(2)}, u32[]{:S(2)}) collective-permute-start(f32[16,512]{1,0:T(8,128)S(1)} %get-tuple-element.15), channel_id=1, source_target_pairs={{0,24},{8,0},{16,8},{24,16},{1,25},{9,1},{17,9},{25,17},{2,26},{10... | collective-permute-start | bytes 98312 | tf_op jit(solution)/shard_map/ppermute | solution.py:261
  73.8 11.7 %collective-permute-start.5 = (f32[48,128]{1,0:T(8,128)S(1)}, f32[48,128]{1,0:T(8,128)S(1)}, u32[]{:S(2)}, u32[]{:S(2)}) collective-permute-start(f32[48,128]{1,0:T(8,128)S(1)} %get-tuple-element.19.total), channel_id=1, source_target_pairs={{0,128},{128,0},{1,129},{129,1},{2,130},{130,2},{3,131},{131,3},{4... | collective-permute-start | bytes 73736 | tf_op jit(solution)/shard_map/ppermute | solution.py:268
  82.9 11.7 %collective-permute-start.6 = (f32[48,128]{1,0:T(8,128)S(1)}, f32[48,128]{1,0:T(8,128)S(1)}, u32[]{:S(2)}, u32[]{:S(2)}) collective-permute-start(f32[48,128]{1,0:T(8,128)S(1)} %get-tuple-element.19.total), channel_id=1, source_target_pairs={{256,128},{257,129},{258,130},{259,131},{260,132},{261,133},{262,1... | collective-permute-start | bytes 73736 | tf_op jit(solution)/shard_map/ppermute | solution.py:269
  83.5 11.1 %collective-permute-start.8 = (f32[48,128]{1,0:T(8,128)S(1)}, f32[48,128]{1,0:T(8,128)S(1)}, u32[]{:S(2)}, u32[]{:S(2)}) collective-permute-start(f32[48,128]{1,0:T(8,128)S(1)} %get-tuple-element.19.total), channel_id=1, source_target_pairs={{256,384},{384,256},{257,385},{385,257},{258,386},{386,258},{259,3... | collective-permute-start | bytes 73736 | tf_op jit(solution)/shard_map/ppermute | solution.py:272
  85.5 10.6 %collective-permute-start.7 = (f32[48,128]{1,0:T(8,128)S(1)}, f32[48,128]{1,0:T(8,128)S(1)}, u32[]{:S(2)}, u32[]{:S(2)}) collective-permute-start(f32[48,128]{1,0:T(8,128)S(1)} %shard_map.46), channel_id=1, source_target_pairs={{128,256},{0,384},{129,257},{1,385},{130,258},{2,386},{131,259},{3... | collective-permute-start | bytes 73736 | tf_op jit(solution)/shard_map/ppermute | solution.py:271
where the time goes:
time: 112 us; the launch traced here: 111 us
  starting transfers between devices  53.1 us (47%)
  blocking collectives  27.9 us (25%)
  waiting for transfers between devices  14 us (12%)
  Pallas kernels  7.54 us (7%)
  local copies, waits for them, and re-layouts  5.85 us (5%)
  other arithmetic  1.97 us (2%)
    all_to_all x2, blocking collectives, exchange(): return lax.all_to_all(value, axes, 0, 0, tiled=True)  27.9 us
    all_to_all x2, starting transfers between devices, exchange(): return lax.all_to_all(value, axes, 0, 0, tiled=True)  18.9 us
    ppermute x3, starting transfers between devices, body(): lax.ppermute(rows[d], 'y', [(i, (i + d) % 4) for i in range(4)])  11.3 us
    ppermute x1, starting transfers between devices, body(): crossed = lax.ppermute(both, 'zh', [(1, 2), (0, 3)])  9.12 us
    ppermute x1, starting transfers between devices, body(): early = lax.ppermute(total, 'zh', [(0, 1), (1, 0)])  9.09 us
    ppermute x1, waiting for transfers between devices, body(): raw_next = lax.ppermute(raw, LAG + PAR, down)  8.89 us
    unnamed x8, local copies, waits for them, and re-layouts  5.85 us
    pallas_call x7, Pallas kernels, call(): pl.pallas_call(kernel, out_shape=out_shape, scratch_shapes=scratch, in_sp...  4.48 us
  transfers between devices with their start and end apart: 11, of which 5 were waited for; matrix products, arithmetic and copies ran while one was open for 2% of the time, Pallas kernels for 6%

commit v1 on v0

--- a/solution.py
+++ b/solution.py
@@ -156,13 +156,13 @@
     whole[...] = summed_rows([parts[x, c] for x in range(4) for c in range(2)])
     place = lax.axis_index("y")
     for d, out in enumerate(outs):
-        out[...] = whole[pl.ds(pl.multiple_of((place + d) % 4 * 16, 16), 16)]
+        out[...] = whole[pl.ds(pl.multiple_of((place ^ d) * 16, 16), 16)]
 
 
 def plane_prefix_kernel(zero_a, zero_b, zero_c, zero_d, one, out, zero):
     place = lax.axis_index("y")
     for d, part in enumerate((zero_a, zero_b, zero_c, zero_d)):
-        zero[(place + 4 - d) % 4] = part[...]
+        zero[place ^ d] = part[...]
     zeros, ones, late = [], [], None
     for lag in range(4):
         zeros.append(zero[lag] if lag == 0 else zeros[-1] + zero[lag])
@@ -258,7 +258,7 @@
     rows = call(add_kernel, (shape(16, 512),) * 4, zero, scratch=(shape(64, 512),))
     zero = [rows[0]]
     for d in range(1, 4):
-        zero.append(lax.ppermute(rows[d], "y", [(i, (i + d) % 4) for i in range(4)]))
+        zero.append(lax.ppermute(rows[d], "y", [(i, i ^ d) for i in range(4)]))
 
     one = call(tile_one_kernel, shape(4, 4, 2, 8, 1152), prior, raw_next, prior_last, raw)
     one = exchange_short(one.reshape(32, 8, 1152), ("y", "x", "core")).reshape(4, 4, 2, 8, 1152)

time: 112 us -> 111 us (level)
  waiting for transfers between devices: 14 us -> 16.1 us
  blocking collectives: 27.9 us -> 26.2 us
    all_to_all x2, blocking collectives: 27.9 us -> 26.2 us  [exchange(): return lax.all_to_all(value, axes, 0, 0, tiled=True)]
    ppermute x3, waiting for transfers between devices: 2.36 us -> 3.86 us  [body(): zero.append(lax.ppermute(rows[d], 'y', [(i, i ^ d) for i in range(4)]))]
  transfers between devices with their start and end apart: 11 -> 11, of which waited for: 5 -> 6; matrix products, arithmetic and copies ran while one was open for 2% -> 2% of each run, Pallas kernels for 6% -> 6%
where the time goes in v1:
time: 111 us
  starting transfers between devices  52.1 us (47%)
  blocking collectives  26.2 us (24%)
  waiting for transfers between devices  16.1 us (15%)
  Pallas kernels  7.53 us (7%)
  local copies, waits for them, and re-layouts  5.85 us (5%)
  other arithmetic  1.97 us (2%)
    all_to_all x2, blocking collectives, exchange(): return lax.all_to_all(value, axes, 0, 0, tiled=True)  26.2 us
    all_to_all x2, starting transfers between devices, exchange(): return lax.all_to_all(value, axes, 0, 0, tiled=True)  18.9 us
    ppermute x3, starting transfers between devices, body(): zero.append(lax.ppermute(rows[d], 'y', [(i, i ^ d) for i in range(4)]))  10.4 us
    ppermute x1, starting transfers between devices, body(): crossed = lax.ppermute(both, 'zh', [(1, 2), (0, 3)])  9.12 us
    ppermute x1, starting transfers between devices, body(): early = lax.ppermute(total, 'zh', [(0, 1), (1, 0)])  9.09 us
    ppermute x1, waiting for transfers between devices, body(): raw_next = lax.ppermute(raw, LAG + PAR, down)  8.89 us
    unnamed x8, local copies, waits for them, and re-layouts  5.85 us
    pallas_call x7, Pallas kernels, call(): pl.pallas_call(kernel, out_shape=out_shape, scratch_shapes=scratch, in_sp...  4.48 us
  transfers between devices with their start and end apart: 11, of which 6 were waited for; matrix products, arithmetic and copies ran while one was open for 2% of the time, Pallas kernels for 6%

profile of v1, /device:TPU:2, one launch (start us, length us, event | category | flops | bytes accessed | tf_op | source)
XLA Modules:
  0.0 110.6 jit_solution(2934780630059489606)
XLA Ops:
  0.6 1.3 %collective-permute-start.3 = (bf16[512,2048]{1,0:T(8,128)(2,1)}, bf16[512,2048]{1,0:T(8,128)(2,1)S(1)}, u32[]{:S(2)}, u32[]{:S(2)}) collective-permute-start(bf16[512,2048]{1,0:T(8,128)(2,1)} %bitcast.10), channel_id=1, source_target_pairs={{8,0},{10,2},{12,4},{14,6},{16,8},{18,10},{20,12},{22,14},{24,16},... | collective-permute-start | bytes 6291464 | tf_op jit(solution)/shard_map/ppermute | solution.py:245
  1.9 2.0 %collective-permute-start.4 = (bf16[512,2048]{1,0:T(8,128)(2,1)}, bf16[512,2048]{1,0:T(8,128)(2,1)}, u32[]{:S(2)}, u32[]{:S(2)}) collective-permute-start(bf16[512,2048]{1,0:T(8,128)(2,1)} %bitcast.12), channel_id=1, source_target_pairs={{1,9},{3,11},{5,13},{7,15},{9,17},{11,19},{13,21},{15,23},{17,25},... | collective-permute-start | bytes 6291464 | tf_op jit(solution)/shard_map/ppermute | solution.py:246
  3.9 3.1 %shard_map.41 = (f32[4,2,8,4224]{3,2,1,0:T(8,128)S(1)}, bf16[512,2048]{1,0:T(8,128)(2,1)S(1)}, bf16[512,2048]{1,0:T(8,128)(2,1)S(1)}) custom-call(bf16[512,2048]{1,0:T(8,128)(2,1)} %bitcast.13, bf16[512,2048]{1,0:T(8,128)(2,1)} %bitcast.11), custom_call_target="tpu_custom_call" | custom-call | tf_op jit(solution)/shard_map/pallas_call | solution.py:249
  7.0 0.0 copy-start
  7.0 1.3 %copy-done = bf16[512,2048]{1,0:T(8,128)(2,1)} copy-done((bf16[512,2048]{1,0:T(8,128)(2,1)}, bf16[512,2048]{1,0:T(8,128)(2,1)S(1)}, u32[]{:S(2)}) %copy-start) | copy-done | bytes 2097176
  8.3 0.0 copy-start.2
  8.3 1.4 %copy-done.2 = bf16[512,2048]{1,0:T(8,128)(2,1)} copy-done((bf16[512,2048]{1,0:T(8,128)(2,1)}, bf16[512,2048]{1,0:T(8,128)(2,1)S(1)}, u32[]{:S(2)}) %copy-start.2) | copy-done | bytes 2097176
  9.7 0.9 convert_element_type.20
  10.5 9.3 %all-to-all-start = ((f16[8,8,4224]{2,1,0:T(8,128)(2,1)}), f16[8,8,4224]{2,1,0:T(8,128)(2,1)S(1)}, u32[]{:S(2)}, u32[]{:S(2)}) async-start(f16[8,8,4224]{2,1,0:T(8,128)(2,1)} %bitcast.2), calls=%async_computation | async-start | bytes 1081344 | tf_op jit(solution)/shard_map/all_to_all | solution.py:233
  19.9 8.9 %collective-permute-done.3.raw_next = bf16[512,2048]{1,0:T(8,128)(2,1)S(1)} collective-permute-done((bf16[512,2048]{1,0:T(8,128)(2,1)}, bf16[512,2048]{1,0:T(8,128)(2,1)S(1)}, u32[]{:S(2)}, u32[]{:S(2)}) %collective-permute-start.3) | collective-permute-done | bytes 2097184 | tf_op jit(solution)/shard_map/ppermute | solution.py:245
  28.8 0.0 collective-permute-done.4.prior_last
  28.8 0.0 copy-start.1
  28.8 1.6 %copy-done.1 = bf16[512,2048]{1,0:T(8,128)(2,1)S(1)} copy-done((bf16[512,2048]{1,0:T(8,128)(2,1)S(1)}, bf16[512,2048]{1,0:T(8,128)(2,1)}, u32[]{:S(2)}) %copy-start.1) | copy-done | bytes 2097176
  30.4 0.0 copy-start.3
  30.4 1.6 %copy-done.3 = bf16[512,2048]{1,0:T(8,128)(2,1)S(1)} copy-done((bf16[512,2048]{1,0:T(8,128)(2,1)S(1)}, bf16[512,2048]{1,0:T(8,128)(2,1)}, u32[]{:S(2)}) %copy-start.3) | copy-done | bytes 2097176
  32.0 3.0 %shard_map.43 = f32[4,4,2,8,1152]{4,3,2,1,0:T(8,128)S(1)} custom-call(bf16[512,2048]{1,0:T(8,128)(2,1)S(1)} %copy-done.1, bf16[512,2048]{1,0:T(8,128)(2,1)S(1)} %collective-permute-done.3.raw_next, bf16[512,2048]{1,0:T(8,128)(2,1)} %collective-permute-done.4.prior_last, bf16[512,2048]{1,0:T(8,128)(2,1)S(1)} %copy-done.3), custom_call_target="tpu_custom_call" | custom-call | tf_op jit(solution)/shard_map/pallas_call | solution.py:28
  35.0 0.9 convert_element_type.22
  35.9 0.0 all-to-all-done
  35.9 9.6 %all-to-all-start.1 = ((f16[32,8,1152]{2,1,0:T(8,128)(2,1)}), f16[32,8,1152]{2,1,0:T(8,128)(2,1)S(1)}, u32[]{:S(2)}, u32[]{:S(2)}) async-start(f16[32,8,1152]{2,1,0:T(8,128)(2,1)} %bitcast.4), calls=%async_computation.1 | async-start | bytes 1179648 | tf_op jit(solution)/shard_map/all_to_all | solution.py:233
  45.5 0.1 convert.2.parts
  45.5 0.1 shard_map.42
  45.6 3.4 %collective-permute-start = (f32[16,512]{1,0:T(8,128)S(1)}, f32[16,512]{1,0:T(8,128)S(1)}, u32[]{:S(2)}, u32[]{:S(2)}) collective-permute-start(f32[16,512]{1,0:T(8,128)S(1)} %get-tuple-element.13), channel_id=1, source_target_pairs={{0,8},{8,0},{16,24},{24,16},{1,9},{9,1},{17,25},{25,17},{2,10},{10... | collective-permute-start | bytes 98312 | tf_op jit(solution)/shard_map/ppermute | solution.py:261
  49.0 4.6 %collective-permute-start.1 = (f32[16,512]{1,0:T(8,128)S(1)}, f32[16,512]{1,0:T(8,128)S(1)}, u32[]{:S(2)}, u32[]{:S(2)}) collective-permute-start(f32[16,512]{1,0:T(8,128)S(1)} %get-tuple-element.14), channel_id=1, source_target_pairs={{0,16},{8,24},{16,0},{24,8},{1,17},{9,25},{17,1},{25,9},{2,18},{10... | collective-permute-start | bytes 98312 | tf_op jit(solution)/shard_map/ppermute | solution.py:261
  53.7 2.4 %collective-permute-start.2 = (f32[16,512]{1,0:T(8,128)S(1)}, f32[16,512]{1,0:T(8,128)S(1)}, u32[]{:S(2)}, u32[]{:S(2)}) collective-permute-start(f32[16,512]{1,0:T(8,128)S(1)} %get-tuple-element.15), channel_id=1, source_target_pairs={{0,24},{8,16},{16,8},{24,0},{1,25},{9,17},{17,9},{25,1},{2,26},{10... | collective-permute-start | bytes 98312 | tf_op jit(solution)/shard_map/ppermute | solution.py:261
  56.1 0.6 all-to-all-done.1
  56.7 0.1 convert.3.one
  56.8 0.0 collective-permute-done.zero_b
  56.8 0.4 collective-permute-done.1.zero_c
  57.2 3.5 %collective-permute-done.2.zero_d = f32[16,512]{1,0:T(8,128)S(1)} collective-permute-done((f32[16,512]{1,0:T(8,128)S(1)}, f32[16,512]{1,0:T(8,128)S(1)}, u32[]{:S(2)}, u32[]{:S(2)}) %collective-permute-start.2) | collective-permute-done | bytes 32800 | tf_op jit(solution)/shard_map/ppermute | solution.py:261
  60.7 0.4 shard_map.44
  61.1 13.6 %all_to_all.20 = f16[4,168,128]{2,1,0:T(8,128)(2,1)S(1)} all-to-all(f16[4,168,128]{2,1,0:T(8,128)(2,1)S(1)} %convert_element_type.24), channel_id=1, replica_groups=mesh['zh'=4,'zl'=4,'y'=4,'x'=4,'core'=2] {'zl'}, dimensions={0} | all-to-all | bytes 344064 | tf_op jit(solution)/shard_map/all_to_all | solution.py:233
  74.7 0.2 shard_map.45
  75.0 9.1 %collective-permute-start.5 = (f32[48,128]{1,0:T(8,128)S(1)}, f32[48,128]{1,0:T(8,128)S(1)}, u32[]{:S(2)}, u32[]{:S(2)}) collective-permute-start(f32[48,128]{1,0:T(8,128)S(1)} %get-tuple-element.19.total), channel_id=1, source_target_pairs={{0,128},{128,0},{1,129},{129,1},{2,130},{130,2},{3,131},{131,3},{4... | collective-permute-start | bytes 73736 | tf_op jit(solution)/shard_map/ppermute | solution.py:268
  84.1 0.7 collective-permute-start.6
  84.8 0.7 collective-permute-start.8
  85.4 1.2 %collective-permute-done.5.other.early = f32[48,128]{1,0:T(8,128)S(1)} collective-permute-done((f32[48,128]{1,0:T(8,128)S(1)}, f32[48,128]{1,0:T(8,128)S(1)}, u32[]{:S(2)}, u32[]{:S(2)}) %collective-permute-start.5) | collective-permute-done | bytes 24608 | tf_op jit(solution)/shard_map/ppermute | solution.py:268
  86.7 9.1 %collective-permute-start.7 = (f32[48,128]{1,0:T(8,128)S(1)}, f32[48,128]{1,0:T(8,128)S(1)}, u32[]{:S(2)}, u32[]{:S(2)}) collective-permute-start(f32[48,128]{1,0:T(8,128)S(1)} %shard_map.46), channel_id=1, source_target_pairs={{128,256},{0,384},{129,257},{1,385},{130,258},{2,386},{131,259},{3... | collective-permute-start | bytes 73736 | tf_op jit(solution)/shard_map/ppermute | solution.py:271
  95.8 0.0 collective-permute-done.6.back
  95.8 0.0 collective-permute-done.8.own
  95.8 1.5 %collective-permute-done.7.crossed = f32[48,128]{1,0:T(8,128)S(1)} collective-permute-done((f32[48,128]{1,0:T(8,128)S(1)}, f32[48,128]{1,0:T(8,128)S(1)}, u32[]{:S(2)}, u32[]{:S(2)}) %collective-permute-start.7) | collective-permute-done | bytes 24608 | tf_op jit(solution)/shard_map/ppermute | solution.py:271
  97.3 12.6 %all_to_all.21.rows = f32[16,32,128]{2,1,0:T(8,128)S(1)} all-to-all(f32[16,32,128]{2,1,0:T(8,128)S(1)} %shard_map.47), channel_id=1, replica_groups=mesh['zh'=4,'zl'=4,'y'=4,'x'=4,'core'=2] {'zl','y'}, dimensions={0} | all-to-all | bytes 524288 | tf_op jit(solution)/shard_map/all_to_all | solution.py:233
  109.9 0.7 shard_map.48
  (4 shorter events, 0.1 us)
Async XLA Ops:
  0.6 28.1 %collective-permute-start.3 = (bf16[512,2048]{1,0:T(8,128)(2,1)}, bf16[512,2048]{1,0:T(8,128)(2,1)S(1)}, u32[]{:S(2)}, u32[]{:S(2)}) collective-permute-start(bf16[512,2048]{1,0:T(8,128)(2,1)} %bitcast.10), channel_id=1, source_target_pairs={{8,0},{10,2},{12,4},{14,6},{16,8},{18,10},{20,12},{22,14},{24,16},... | collective-permute-start | bytes 6291464 | tf_op jit(solution)/shard_map/ppermute | solution.py:245
  1.9 26.8 %collective-permute-start.4 = (bf16[512,2048]{1,0:T(8,128)(2,1)}, bf16[512,2048]{1,0:T(8,128)(2,1)}, u32[]{:S(2)}, u32[]{:S(2)}) collective-permute-start(bf16[512,2048]{1,0:T(8,128)(2,1)} %bitcast.12), channel_id=1, source_target_pairs={{1,9},{3,11},{5,13},{7,15},{9,17},{11,19},{13,21},{15,23},{17,25},... | collective-permute-start | bytes 6291464 | tf_op jit(solution)/shard_map/ppermute | solution.py:246
  7.0 1.3 %copy-start = (bf16[512,2048]{1,0:T(8,128)(2,1)}, bf16[512,2048]{1,0:T(8,128)(2,1)S(1)}, u32[]{:S(2)}) copy-start(bf16[512,2048]{1,0:T(8,128)(2,1)S(1)} %get-tuple-element.16.prior) | copy-start | bytes 6291460
  8.3 1.4 %copy-start.2 = (bf16[512,2048]{1,0:T(8,128)(2,1)}, bf16[512,2048]{1,0:T(8,128)(2,1)S(1)}, u32[]{:S(2)}) copy-start(bf16[512,2048]{1,0:T(8,128)(2,1)S(1)} %get-tuple-element.17.raw) | copy-start | bytes 6291460
  10.5 25.4 %all-to-all-start = ((f16[8,8,4224]{2,1,0:T(8,128)(2,1)}), f16[8,8,4224]{2,1,0:T(8,128)(2,1)S(1)}, u32[]{:S(2)}, u32[]{:S(2)}) async-start(f16[8,8,4224]{2,1,0:T(8,128)(2,1)} %bitcast.2), calls=%async_computation | async-start | bytes 1081344 | tf_op jit(solution)/shard_map/all_to_all | solution.py:233
  28.8 1.6 %copy-start.1 = (bf16[512,2048]{1,0:T(8,128)(2,1)S(1)}, bf16[512,2048]{1,0:T(8,128)(2,1)}, u32[]{:S(2)}) copy-start(bf16[512,2048]{1,0:T(8,128)(2,1)} %copy-done) | copy-start | bytes 6291460
  30.4 1.6 %copy-start.3 = (bf16[512,2048]{1,0:T(8,128)(2,1)S(1)}, bf16[512,2048]{1,0:T(8,128)(2,1)}, u32[]{:S(2)}) copy-start(bf16[512,2048]{1,0:T(8,128)(2,1)} %copy-done.2) | copy-start | bytes 6291460
  35.9 20.8 %all-to-all-start.1 = ((f16[32,8,1152]{2,1,0:T(8,128)(2,1)}), f16[32,8,1152]{2,1,0:T(8,128)(2,1)S(1)}, u32[]{:S(2)}, u32[]{:S(2)}) async-start(f16[32,8,1152]{2,1,0:T(8,128)(2,1)} %bitcast.4), calls=%async_computation.1 | async-start | bytes 1179648 | tf_op jit(solution)/shard_map/all_to_all | solution.py:233
  45.6 11.2 %collective-permute-start = (f32[16,512]{1,0:T(8,128)S(1)}, f32[16,512]{1,0:T(8,128)S(1)}, u32[]{:S(2)}, u32[]{:S(2)}) collective-permute-start(f32[16,512]{1,0:T(8,128)S(1)} %get-tuple-element.13), channel_id=1, source_target_pairs={{0,8},{8,0},{16,24},{24,16},{1,9},{9,1},{17,25},{25,17},{2,10},{10... | collective-permute-start | bytes 98312 | tf_op jit(solution)/shard_map/ppermute | solution.py:261
  49.0 8.2 %collective-permute-start.1 = (f32[16,512]{1,0:T(8,128)S(1)}, f32[16,512]{1,0:T(8,128)S(1)}, u32[]{:S(2)}, u32[]{:S(2)}) collective-permute-start(f32[16,512]{1,0:T(8,128)S(1)} %get-tuple-element.14), channel_id=1, source_target_pairs={{0,16},{8,24},{16,0},{24,8},{1,17},{9,25},{17,1},{25,9},{2,18},{10... | collective-permute-start | bytes 98312 | tf_op jit(solution)/shard_map/ppermute | solution.py:261
  53.7 7.0 %collective-permute-start.2 = (f32[16,512]{1,0:T(8,128)S(1)}, f32[16,512]{1,0:T(8,128)S(1)}, u32[]{:S(2)}, u32[]{:S(2)}) collective-permute-start(f32[16,512]{1,0:T(8,128)S(1)} %get-tuple-element.15), channel_id=1, source_target_pairs={{0,24},{8,16},{16,8},{24,0},{1,25},{9,17},{17,9},{25,1},{2,26},{10... | collective-permute-start | bytes 98312 | tf_op jit(solution)/shard_map/ppermute | solution.py:261
  75.0 11.7 %collective-permute-start.5 = (f32[48,128]{1,0:T(8,128)S(1)}, f32[48,128]{1,0:T(8,128)S(1)}, u32[]{:S(2)}, u32[]{:S(2)}) collective-permute-start(f32[48,128]{1,0:T(8,128)S(1)} %get-tuple-element.19.total), channel_id=1, source_target_pairs={{0,128},{128,0},{1,129},{129,1},{2,130},{130,2},{3,131},{131,3},{4... | collective-permute-start | bytes 73736 | tf_op jit(solution)/shard_map/ppermute | solution.py:268
  84.1 11.7 %collective-permute-start.6 = (f32[48,128]{1,0:T(8,128)S(1)}, f32[48,128]{1,0:T(8,128)S(1)}, u32[]{:S(2)}, u32[]{:S(2)}) collective-permute-start(f32[48,128]{1,0:T(8,128)S(1)} %get-tuple-element.19.total), channel_id=1, source_target_pairs={{256,128},{257,129},{258,130},{259,131},{260,132},{261,133},{262,1... | collective-permute-start | bytes 73736 | tf_op jit(solution)/shard_map/ppermute | solution.py:269
  84.8 11.1 %collective-permute-start.8 = (f32[48,128]{1,0:T(8,128)S(1)}, f32[48,128]{1,0:T(8,128)S(1)}, u32[]{:S(2)}, u32[]{:S(2)}) collective-permute-start(f32[48,128]{1,0:T(8,128)S(1)} %get-tuple-element.19.total), channel_id=1, source_target_pairs={{256,384},{384,256},{257,385},{385,257},{258,386},{386,258},{259,3... | collective-permute-start | bytes 73736 | tf_op jit(solution)/shard_map/ppermute | solution.py:272
  86.7 10.6 %collective-permute-start.7 = (f32[48,128]{1,0:T(8,128)S(1)}, f32[48,128]{1,0:T(8,128)S(1)}, u32[]{:S(2)}, u32[]{:S(2)}) collective-permute-start(f32[48,128]{1,0:T(8,128)S(1)} %shard_map.46), channel_id=1, source_target_pairs={{128,256},{0,384},{129,257},{1,385},{130,258},{2,386},{131,259},{3... | collective-permute-start | bytes 73736 | tf_op jit(solution)/shard_map/ppermute | solution.py:271
